TPU v7x, 32 devices: a whole 2x2x4 slice. The times are simulated.
32 devices in a mesh: gx: 4 (over y, x), gy: 4 (over z), gz: 2 (over core).
Axes of the slice: x: 2, y: 2, z: 4, core: 2. Of those that a mesh axis runs over, the one named last changes fastest.
Arguments:
- provisional: float32 [9, 128, 64, 256], P(None, 'gx', 'gy', 'gz'), may hold values from -6 to 6
- cut_flag: int32 [128, 64, 256], P('gx', 'gy', 'gz'), may hold values from 0 to 1, as said below
- cut_code: int32 [128, 64, 256], P('gx', 'gy', 'gz'), may hold values from 0 to 134217727
- volume_level: int32 [128, 64, 256], P('gx', 'gy', 'gz'), may hold values from 1 to 256
- area_level: int32 [128, 64, 256], P('gx', 'gy', 'gz'), may hold values from 64 to 256
Outputs:
- redistributed: float32 [9, 128, 64, 256], P(None, 'gx', 'gy', 'gz')
- species_change: float32 [9], replicated
Inputs may be any that keep to these rules, and one draw needn't show every extreme that they name: cut_flag marks the cells crossed by one closed embedded surface.
All inputs are finite; a program needn't handle non-finite values.
Results may differ from a plain program's by a relative error of at most 0.00002.
Values sent between devices are 32-bit elements; how exact they have to be, the bound alone decides.
A program may use at most 128 MiB of HBM per device.

v0:
```python
import math
import jax
import jax.numpy as jnp
from jax import lax
from jax.sharding import PartitionSpec as P

CENTER = 8192
OFFSETS = [(a, b, c) for a in (-1, 0, 1) for b in (-1, 0, 1) for c in (-1, 0, 1)]


def padded(cells, sides, width):
    for axis, dim in sides:
        count = lax.axis_size(axis)
        ends = count - 1
        head = lax.slice_in_dim(cells, 0, width, axis=dim)
        tail = lax.slice_in_dim(cells, cells.shape[dim] - width, cells.shape[dim], axis=dim)
        cells = jnp.concatenate(
            [
                lax.ppermute(tail, axis, [(i, (i + 1) % count) for i in range(ends)]),
                cells,
                lax.ppermute(head, axis, [((i + 1) % count, i) for i in range(ends)]),
            ],
            axis=dim,
        )
    return cells


def window(values, a, b, c, margin, border):
    extent_x = values.shape[-3] - 2 * border + 2 * margin
    extent_y = values.shape[-2] - 2 * border + 2 * margin
    extent_z = values.shape[-1] - 2 * border + 2 * margin
    start_x = border - margin + a
    start_y = border - margin + b
    start_z = border - margin + c
    return values[
        ...,
        start_x : start_x + extent_x,
        start_y : start_y + extent_y,
        start_z : start_z + extent_z,
    ]


def member(codes, position):
    return (codes >> position & 1).astype(jnp.float32)


def per_device(provisional, cut_flag, cut_code, volume_level, area_level):
    is_cut = cut_flag == 1
    stacked = jnp.stack(
        [
            jnp.where(is_cut, cut_code | CENTER, CENTER),
            jnp.where(is_cut, volume_level, 256),
            jnp.where(is_cut, area_level, 256),
        ]
    )
    border = 2
    grown = padded(stacked, (("gx", 1), ("gy", 2), ("gz", 3)), border)
    code_all = grown[0] | CENTER
    volume_all = grown[1].astype(jnp.float32) / 256.0
    face_all = grown[2].astype(jnp.float32) / 256.0
    margin = border - 1
    counted = jnp.zeros(window(code_all, 0, 0, 0, margin, border).shape, jnp.float32)
    for position, (a, b, c) in enumerate(OFFSETS):
        counted = counted + member(window(code_all, -a, -b, -c, margin, border), position)
    volume_near = window(volume_all, 0, 0, 0, margin, border)
    face_near = window(face_all, 0, 0, 0, margin, border)
    weights = volume_near / counted
    portions = volume_near * face_near / counted
    scaling = window(face_all, 0, 0, 0, 0, border) / window(counted, 0, 0, 0, 0, margin)
    volume_mid = window(volume_all, 0, 0, 0, 0, border)
    carried = padded(
        window(weights, 0, 0, 0, 0, 1)[None] * provisional, (("gx", 1), ("gy", 2), ("gz", 3)), 1
    )
    carry_border = 1
    inner_margin = 0
    code_inner = window(code_all, 0, 0, 0, inner_margin, border)
    beyond = (window(grown[1], 0, 0, 0, inner_margin, border) == 0).astype(jnp.float32)
    amounts = jnp.zeros(window(carried, 0, 0, 0, inner_margin, carry_border).shape, jnp.float32)
    gathered = jnp.zeros(code_inner.shape, jnp.float32)
    for position, (a, b, c) in enumerate(OFFSETS):
        present = member(code_inner, position)
        amounts = amounts + present * window(carried, a, b, c, inner_margin, carry_border)
        gathered = gathered + present * window(portions, a, b, c, inner_margin, margin)
    quotas = amounts / (gathered + beyond)
    quotas = padded(quotas, (("gx", 1), ("gy", 2), ("gz", 3)), 1)
    summed = jnp.zeros(provisional.shape, jnp.float32)
    for position, (a, b, c) in enumerate(OFFSETS):
        summed = summed + member(window(code_all, -a, -b, -c, 0, border), position) * window(
            quotas, -a, -b, -c, 0, 1
        )
    redistributed = scaling * summed
    cell_count = (
        provisional.shape[1]
        * provisional.shape[2]
        * provisional.shape[3]
        * lax.axis_size("gx")
        * lax.axis_size("gy")
        * lax.axis_size("gz")
    )
    local_sums = jnp.sum(volume_mid[None] * redistributed, axis=(1, 2, 3))
    species_change = lax.psum(local_sums, ("gx", "gy", "gz")) / math.sqrt(cell_count)
    return (redistributed, species_change)


def solution(mesh):
    in_specs = (
        P(None, "gx", "gy", "gz"),
        P("gx", "gy", "gz"),
        P("gx", "gy", "gz"),
        P("gx", "gy", "gz"),
        P("gx", "gy", "gz"),
    )
    out_specs = (P(None, "gx", "gy", "gz"), P())
    return jax.shard_map(
        per_device, mesh=mesh, in_specs=in_specs, out_specs=out_specs, check_vma=False
    )
```

profile of v0, /device:TPU:0, one launch (start us, length us, event | category | flops | bytes accessed | tf_op | source)
XLA Modules:
  0.0 276.7 jit_solution(5008713613444649050)
XLA Ops:
  0.6 1.1 select_bitcast_fusion.2
  1.7 1.1 select_bitcast_fusion.1
  2.8 4.9 %collective-permute-start = (s32[3,2,16,128]{3,2,1,0:T(8,128)S(1)}, s32[3,2,16,128]{3,2,1,0:T(8,128)S(1)}, u32[]{:S(2)}, u32[]{:S(2)}) collective-permute-start(s32[3,2,16,128]{3,2,1,0:T(8,128)S(1)} %get-tuple-element.91), channel_id=1, source_target_pairs={{0,8},{8,16},{16,24},{1,9},{9,17},{17,25},{2,10},{10,18},{18,26},{... | collective-permute-start | bytes 147464 | tf_op jit(solution)/shard_map/ppermute | solution.py:19
  7.7 1.3 collective-permute-start.1
  9.0 0.4 collective-permute-done
  9.4 4.2 %collective-permute-done.1 = s32[3,2,16,128]{3,2,1,0:T(8,128)S(1)} collective-permute-done((s32[3,2,16,128]{3,2,1,0:T(8,128)S(1)}, s32[3,2,16,128]{3,2,1,0:T(8,128)S(1)}, u32[]{:S(2)}, u32[]{:S(2)}) %collective-permute-start.1) | collective-permute-done | bytes 49184 | tf_op jit(solution)/shard_map/ppermute | solution.py:21
  13.8 3.5 %collective-permute-start.2 = (s32[3,36,2,128]{3,2,1,0:T(2,128)S(1)}, s32[3,36,2,128]{3,2,1,0:T(2,128)S(1)}, u32[]{:S(2)}, u32[]{:S(2)}) collective-permute-start(s32[3,36,2,128]{3,2,1,0:T(2,128)S(1)} %get-tuple-element.87), channel_id=1, source_target_pairs={{0,2},{2,4},{4,6},{1,3},{3,5},{5,7},{8,10},{10,12},{12,14},{9,11},... | collective-permute-start | bytes 331784 | tf_op jit(solution)/shard_map/ppermute | solution.py:19
  17.3 1.3 collective-permute-start.3
  18.6 1.0 collective-permute-done.2
  19.6 4.3 %collective-permute-done.3 = s32[3,36,2,128]{3,2,1,0:T(2,128)S(1)} collective-permute-done((s32[3,36,2,128]{3,2,1,0:T(2,128)S(1)}, s32[3,36,2,128]{3,2,1,0:T(2,128)S(1)}, u32[]{:S(2)}, u32[]{:S(2)}) %collective-permute-start.3) | collective-permute-done | bytes 110624 | tf_op jit(solution)/shard_map/ppermute | solution.py:21
  23.9 0.6 copy-done.4
  25.2 1.1 copy.193
  26.3 1.3 collective-permute-start.4
  27.6 0.5 copy.194
  28.2 1.3 collective-permute-start.5
  29.5 0.6 copy.195
  30.1 1.3 collective-permute-done.5
  31.4 1.5 copy.196
  32.9 4.2 %pad_add_fusion = s32[3,36,20,132]{3,2,1,0:T(8,128)S(1)} fusion(s32[3,36,20,2]{3,2,1,0:T(8,128)S(1)} %copy.196, s32[3,36,2,128]{3,2,1,0:T(2,128)} %copy-done.4, s32[3,2,16,128]{3,2,1,0:T(8,128)} %copy-done.6, s32[1,32,16,128]{3,2,1,0:T(8,128)S(1)} %get-tuple-element.94, s32[1,32,16,128]{3,2,1,0:T(8,128)S(1)} %get-tuple-element.93, ...), kind=kLoop, calls=%fused_computation.10 | loop fusion | flops 2280960 | bytes 2280960 | tf_op jit(solution)/shard_map/concatenate | solution.py:17
  37.6 3.0 %fusion.220 = (f32[32,16,128]{2,1,0:T(8,128)}, f32[32,16,128]{2,1,0:T(8,128)}, f32[32,16,128]{2,1,0:T(8,128)}, f32[32,16,128]{2,1,0:T(8,128)}, f32[32,16,128]{2,...) fusion(s32[36,20,132]{2,1,0:T(8,128)S(1)} %get-tuple-element.19), kind=kLoop, calls=%fused_computation.373 | loop fusion | flops 3735552 | bytes 5505024 | tf_op jit(solution)/shard_map/convert_element_type | solution.py:44
  40.6 4.8 %fusion.61 = (f32[34,18,130]{2,1,0:T(8,128)S(1)}, f32[34,18,130]{2,1,0:T(8,128)S(1)}) fusion(f32[36,20,132]{2,1,0:T(8,128)S(1)} %fusion.60, f32[36,20,132]{2,1,0:T(8,128)S(1)} %convert_multiply_fusion, s32[36,20,132]{2,1,0:T(8,128)S(1)} %get-tuple-element.19), kind=kLoop, calls=%fused_computation.132 | loop fusion | flops 8672040 | bytes 9865440 | tf_op jit(solution)/shard_map/div | solution.py:68
  45.4 1.0 slice_divide_fusion.1
  46.6 4.3 %collective-permute-start.6 = (f32[9,1,16,128]{3,2,1,0:T(8,128)S(1)}, f32[9,1,16,128]{3,2,1,0:T(8,128)S(1)}, u32[]{:S(2)}, u32[]{:S(2)}) collective-permute-start(f32[9,1,16,128]{3,2,1,0:T(8,128)S(1)} %get-tuple-element.30), channel_id=1, source_target_pairs={{0,8},{8,16},{16,24},{1,9},{9,17},{17,25},{2,10},{10,18},{18,26},{... | collective-permute-start | bytes 221192 | tf_op jit(solution)/shard_map/ppermute | solution.py:19
  50.9 1.3 collective-permute-start.7
  52.2 2.3 fusion.193
  54.5 3.1 %fusion.191 = (f32[32,16,128]{2,1,0:T(8,128)}, f32[32,16,128]{2,1,0:T(8,128)}, f32[32,16,128]{2,1,0:T(8,128)}, f32[32,16,128]{2,1,0:T(8,128)}, f32[32,16,128]{2,...) fusion(s32[36,20,132]{2,1,0:T(8,128)S(1)} %get-tuple-element.19), kind=kLoop, calls=%fused_computation.314 | loop fusion | flops 3735552 | bytes 8126464 | tf_op jit(solution)/shard_map/convert_element_type | solution.py:44
  57.9 1.3 collective-permute-start.9
  59.2 4.7 %collective-permute-start.8 = (f32[9,34,1,128]{3,1,2,0:T(8,128)S(1)}, f32[9,34,1,128]{3,1,2,0:T(8,128)S(1)}, u32[]{:S(2)}, u32[]{:S(2)}) collective-permute-start(f32[9,34,1,128]{3,1,2,0:T(8,128)S(1)} %copy.197), channel_id=1, source_target_pairs={{0,2},{2,4},{4,6},{1,3},{3,5},{5,7},{8,10},{10,12},{12,14},{9,11},... | collective-permute-start | bytes 470024 | tf_op jit(solution)/shard_map/ppermute | solution.py:19
  63.9 3.0 %fusion.189 = (f32[32,16,128]{2,1,0:T(8,128)}, f32[32,16,128]{2,1,0:T(8,128)}, f32[32,16,128]{2,1,0:T(8,128)}, f32[32,16,128]{2,1,0:T(8,128)}, f32[32,16,128]{2,...) fusion(s32[36,20,132]{2,1,0:T(8,128)S(1)} %get-tuple-element.19), kind=kLoop, calls=%fused_computation.311 | loop fusion | flops 2949120 | bytes 7864320 | tf_op jit(solution)/shard_map/convert_element_type | solution.py:44
  67.1 0.5 collective-permute-done.8
  67.8 0.6 pad_maximum_fusion.2
  68.4 4.2 %fusion.224 = (f32[9,34,18,1]{3,2,1,0:T(8,128)}, f32[9,34,18,1]{3,2,1,0:T(8,128)}) fusion(f32[9,34,18,128]{3,2,1,0:T(8,128)S(1)} %pad_maximum_fusion.2), kind=kLoop, calls=%fused_computation.422 | loop fusion | bytes 88128 | tf_op jit(solution)/shard_map/slice | solution.py:16
  72.6 3.5 %copy.201 = f32[9,34,18,1]{1,2,3,0:T(8,128)S(1)} copy(f32[9,34,18,1]{3,2,1,0:T(8,128)} %get-tuple-element.12) | data formatting | bytes 44064 | tf_op jit(solution)/shard_map/slice | solution.py:16
  76.1 3.5 %copy.204 = f32[9,34,18,1]{1,2,3,0:T(8,128)S(1)} copy(f32[9,34,18,1]{3,2,1,0:T(8,128)} %get-tuple-element.13) | data formatting | bytes 44064 | tf_op jit(solution)/shard_map/slice | solution.py:15
  79.7 1.3 collective-permute-start.11
  81.0 3.7 %collective-permute-start.10 = (f32[9,34,18,1]{1,2,3,0:T(8,128)S(1)}, f32[9,34,18,1]{1,2,3,0:T(8,128)}, u32[]{:S(2)}, u32[]{:S(2)}) collective-permute-start(f32[9,34,18,1]{1,2,3,0:T(8,128)S(1)} %copy.201), channel_id=1, source_target_pairs={{0,1},{2,3},{4,5},{6,7},{8,9},{10,11},{12,13},{14,15},{16,17},{18,... | collective-permute-start | bytes 66104 | tf_op jit(solution)/shard_map/ppermute | solution.py:19
  84.7 3.7 %maximum_maximum_fusion.2 = (f32[9,34,17,128]{3,2,1,0:T(8,128)}, f32[9,34,17,128]{3,2,1,0:T(8,128)}) fusion(f32[9,1,16,128]{3,2,1,0:T(8,128)S(1)} %collective-permute-done.7, f32[9,32,16,128]{3,2,1,0:T(8,128)S(1)} %broadcast_multiply_fusion, f32[9,1,16,128]{3,2,1,0:T(8,128)S(1)} %collective-permute-done.6, f32[9,34,1,128]{3,2,1,0:T(1,128)S(1)} %copy.199, ...), kind=kLoop, calls=%fused_computation.5 | loop fusion | flops 3995136 | bytes 8146944 | tf_op jit(solution)/shard_map/concatenate | solution.py:17
  88.4 3.9 %copy.202 = f32[9,34,18,1]{3,2,1,0:T(8,128)} copy(f32[9,34,18,1]{1,2,3,0:T(8,128)} %collective-permute-done.10) | data formatting | bytes 44064 | tf_op jit(solution)/shard_map/ppermute | solution.py:19
  92.3 3.2 %copy.205 = f32[9,34,18,1]{3,2,1,0:T(8,128)} copy(f32[9,34,18,1]{1,2,3,0:T(8,128)S(1)} %collective-permute-done.11) | data formatting | bytes 44064 | tf_op jit(solution)/shard_map/ppermute | solution.py:21
  95.5 10.9 %maximum_maximum_fusion = (f32[9,34,18,129]{3,2,1,0:T(8,128)S(1)}, f32[9,34,18,129]{3,2,1,0:T(8,128)}) fusion(f32[9,34,1,128]{3,2,1,0:T(1,128)S(1)} %copy.200, f32[9,1,16,128]{3,2,1,0:T(8,128)S(1)} %collective-permute-done.7, f32[9,32,16,128]{3,2,1,0:T(8,128)} %copy-done.1, f32[9,1,16,128]{3,2,1,0:T(8,128)S(1)} %collective-permute-done.6, ...), kind=kLoop, calls=%fused_computation | loop fusion | flops 7105320 | bytes 8548416 | tf_op jit(solution)/shard_map/concatenate | solution.py:17
  106.4 36.9 %fusion.30 = f32[9,32,16,128]{3,2,1,0:T(8,128)} fusion(f32[9,34,18,129]{3,2,1,0:T(8,128)} %get-tuple-element.17, f32[9,34,17,128]{3,2,1,0:T(8,128)} %get-tuple-element.25, f32[9,34,18,129]{3,2,1,0:T(8,128)S(1)} %get-tuple-element.16, f32[9,1,16,128]{3,2,1,0:T(8,128)S(1)} %collective-permute-done.7, f32[9,32,16,128]{3,2,1,0:T(8,128)} %copy-done.1, ...), kind=kLoop, calls=%fused_computation.68 | loop fusion | flops 33030144 | bytes 68829184 | tf_op jit(solution)/shard_map/div | solution.py:84
  143.3 0.9 fusion.225
  144.3 4.4 %collective-permute-start.12 = (f32[9,1,16,128]{3,2,1,0:T(8,128)S(1)}, f32[9,1,16,128]{3,2,1,0:T(8,128)S(1)}, u32[]{:S(2)}, u32[]{:S(2)}) collective-permute-start(f32[9,1,16,128]{3,2,1,0:T(8,128)S(1)} %get-tuple-element.28), channel_id=1, source_target_pairs={{0,8},{8,16},{16,24},{1,9},{9,17},{17,25},{2,10},{10,18},{18,26},{... | collective-permute-start | bytes 221192 | tf_op jit(solution)/shard_map/ppermute | solution.py:19
  148.7 1.3 collective-permute-start.13
  150.0 0.7 collective-permute-done.12
  150.7 4.3 %collective-permute-done.13 = f32[9,1,16,128]{3,2,1,0:T(8,128)S(1)} collective-permute-done((f32[9,1,16,128]{3,2,1,0:T(8,128)S(1)}, f32[9,1,16,128]{3,2,1,0:T(8,128)S(1)}, u32[]{:S(2)}, u32[]{:S(2)}) %collective-permute-start.13) | collective-permute-done | bytes 73760 | tf_op jit(solution)/shard_map/ppermute | solution.py:21
  155.0 1.9 pad_maximum_fusion.12
  156.9 1.3 collective-permute-start.15
  158.2 5.2 %collective-permute-start.14 = (f32[9,34,1,128]{3,1,2,0:T(8,128)S(1)}, f32[9,34,1,128]{3,1,2,0:T(8,128)S(1)}, u32[]{:S(2)}, u32[]{:S(2)}) collective-permute-start(f32[9,34,1,128]{3,1,2,0:T(8,128)S(1)} %copy.207), channel_id=1, source_target_pairs={{0,2},{2,4},{4,6},{1,3},{3,5},{5,7},{8,10},{10,12},{12,14},{9,11},... | collective-permute-start | bytes 470024 | tf_op jit(solution)/shard_map/ppermute | solution.py:19
  163.5 2.0 slice.847
  165.6 0.7 collective-permute-done.14
  166.4 0.6 pad_maximum_fusion.4
  167.1 4.4 %fusion.223 = (f32[9,34,18,1]{3,2,1,0:T(8,128)}, f32[9,34,18,1]{3,2,1,0:T(8,128)}) fusion(f32[9,34,18,128]{3,2,1,0:T(8,128)S(1)} %pad_maximum_fusion.4), kind=kLoop, calls=%fused_computation.421 | loop fusion | bytes 88128 | tf_op jit(solution)/shard_map/slice | solution.py:15
  171.4 3.5 %copy.211 = f32[9,34,18,1]{1,2,3,0:T(8,128)S(1)} copy(f32[9,34,18,1]{3,2,1,0:T(8,128)} %get-tuple-element.10) | data formatting | bytes 44064 | tf_op jit(solution)/shard_map/slice | solution.py:15
  175.0 3.5 %copy.214 = f32[9,34,18,1]{1,2,3,0:T(8,128)S(1)} copy(f32[9,34,18,1]{3,2,1,0:T(8,128)} %get-tuple-element.11) | data formatting | bytes 44064 | tf_op jit(solution)/shard_map/slice | solution.py:16
  178.5 1.3 collective-permute-start.17
  179.8 1.3 collective-permute-start.16
  181.1 3.8 %pad_maximum_fusion.5 = (f32[9,34,17,128]{3,2,1,0:T(8,128)}, f32[9,34,17,128]{3,2,1,0:T(8,128)}) fusion(f32[9,34,1,128]{3,2,1,0:T(1,128)S(1)} %copy.210, f32[9,1,16,128]{3,2,1,0:T(8,128)S(1)} %collective-permute-done.13, f32[9,32,16,128]{3,2,1,0:T(8,128)S(1)} %copy-done, f32[9,1,16,128]{3,2,1,0:T(8,128)S(1)} %collective-permute-done.12, ...), kind=kLoop, calls=%fused_computation.8 | loop fusion | flops 3995136 | bytes 8146944 | tf_op jit(solution)/shard_map/concatenate | solution.py:17
  185.0 4.0 %copy.212 = f32[9,34,18,1]{3,2,1,0:T(8,128)} copy(f32[9,34,18,1]{1,2,3,0:T(8,128)} %collective-permute-done.16) | data formatting | bytes 44064 | tf_op jit(solution)/shard_map/ppermute | solution.py:21
  189.0 3.2 %copy.215 = f32[9,34,18,1]{3,2,1,0:T(8,128)} copy(f32[9,34,18,1]{1,2,3,0:T(8,128)S(1)} %collective-permute-done.17) | data formatting | bytes 44064 | tf_op jit(solution)/shard_map/ppermute | solution.py:19
  192.2 11.2 %pad_maximum_fusion.1 = (f32[9,34,18,129]{3,2,1,0:T(8,128)S(1)}, f32[9,34,18,129]{3,2,1,0:T(8,128)}) fusion(f32[9,34,18,1]{3,2,1,0:T(8,128)} %copy.212, f32[9,34,1,128]{3,2,1,0:T(1,128)S(1)} %copy.210, f32[9,1,16,128]{3,2,1,0:T(8,128)S(1)} %collective-permute-done.13, f32[9,32,16,128]{3,2,1,0:T(8,128)} %fusion.30, ...), kind=kLoop, calls=%fused_computation.2 | loop fusion | flops 7105320 | bytes 8548416 | tf_op jit(solution)/shard_map/concatenate | solution.py:17
  203.4 29.8 %multiply_reduce_fusion = (f32[9]{0:T(128)S(1)}, f32[9,32,16,128]{3,2,1,0:T(8,128)}) fusion(f32[32,16,128]{2,1,0:T(8,128)} %slice.847, f32[9,34,18,129]{3,2,1,0:T(8,128)} %get-tuple-element.15, f32[32,16,128]{2,1,0:T(8,128)} %get-tuple-element.62, f32[9,34,17,128]{3,2,1,0:T(8,128)} %get-tuple-element.21, f32[32,16,128]{2,1,0:T(8,128)} %get-tuple-element.63, ...), kind=kLoop, calls=%fused_computation.121 | loop fusion | flops 34209784 | bytes 69091360 | tf_op jit(solution)/shard_map/reduce_sum | solution.py:100
  233.2 43.0 %psum.7 = f32[9]{0:T(128)S(1)} all-reduce(f32[9]{0:T(128)S(1)} %get-tuple-element.4), channel_id=1, replica_groups=mesh['gx'=4,'gy'=4,'gz'=2] {'gx','gy','gz'}, use_global_device_ids=true, to_apply=%region_1.2 | all-reduce | flops 9 | bytes 72 | tf_op jit(solution)/shard_map/psum | solution.py:101
  276.2 0.5 broadcast_multiply_fusion.1
  (41 shorter events, 2.4 us)
Async XLA Ops:
  2.8 6.6 %collective-permute-start = (s32[3,2,16,128]{3,2,1,0:T(8,128)S(1)}, s32[3,2,16,128]{3,2,1,0:T(8,128)S(1)}, u32[]{:S(2)}, u32[]{:S(2)}) collective-permute-start(s32[3,2,16,128]{3,2,1,0:T(8,128)S(1)} %get-tuple-element.91), channel_id=1, source_target_pairs={{0,8},{8,16},{16,24},{1,9},{9,17},{17,25},{2,10},{10,18},{18,26},{... | collective-permute-start | bytes 147464 | tf_op jit(solution)/shard_map/ppermute | solution.py:19
  7.7 6.0 %collective-permute-start.1 = (s32[3,2,16,128]{3,2,1,0:T(8,128)S(1)}, s32[3,2,16,128]{3,2,1,0:T(8,128)S(1)}, u32[]{:S(2)}, u32[]{:S(2)}) collective-permute-start(s32[3,2,16,128]{3,2,1,0:T(8,128)S(1)} %get-tuple-element.92), channel_id=1, source_target_pairs={{8,0},{16,8},{24,16},{9,1},{17,9},{25,17},{10,2},{18,10},{26,18},{... | collective-permute-start | bytes 147464 | tf_op jit(solution)/shard_map/ppermute | solution.py:21
  9.4 14.5 %copy-start.5 = (s32[3,2,16,128]{3,2,1,0:T(8,128)}, s32[3,2,16,128]{3,2,1,0:T(8,128)S(1)}, u32[]{:S(2)}) copy-start(s32[3,2,16,128]{3,2,1,0:T(8,128)S(1)} %collective-permute-done) | copy-start | bytes 147460
  13.7 10.2 %copy-start.6 = (s32[3,2,16,128]{3,2,1,0:T(8,128)}, s32[3,2,16,128]{3,2,1,0:T(8,128)S(1)}, u32[]{:S(2)}) copy-start(s32[3,2,16,128]{3,2,1,0:T(8,128)S(1)} %collective-permute-done.1) | copy-start | bytes 147460
  13.8 5.8 %collective-permute-start.2 = (s32[3,36,2,128]{3,2,1,0:T(2,128)S(1)}, s32[3,36,2,128]{3,2,1,0:T(2,128)S(1)}, u32[]{:S(2)}, u32[]{:S(2)}) collective-permute-start(s32[3,36,2,128]{3,2,1,0:T(2,128)S(1)} %get-tuple-element.87), channel_id=1, source_target_pairs={{0,2},{2,4},{4,6},{1,3},{3,5},{5,7},{8,10},{10,12},{12,14},{9,11},... | collective-permute-start | bytes 331784 | tf_op jit(solution)/shard_map/ppermute | solution.py:19
  17.3 6.6 %collective-permute-start.3 = (s32[3,36,2,128]{3,2,1,0:T(2,128)S(1)}, s32[3,36,2,128]{3,2,1,0:T(2,128)S(1)}, u32[]{:S(2)}, u32[]{:S(2)}) collective-permute-start(s32[3,36,2,128]{3,2,1,0:T(2,128)S(1)} %get-tuple-element.88), channel_id=1, source_target_pairs={{2,0},{4,2},{6,4},{3,1},{5,3},{7,5},{10,8},{12,10},{14,12},{11,9},... | collective-permute-start | bytes 331784 | tf_op jit(solution)/shard_map/ppermute | solution.py:21
  23.9 0.6 copy-start.4
  26.3 3.1 %collective-permute-start.4 = (s32[3,36,20,2]{1,3,2,0:T(2,128)}, s32[3,36,20,2]{1,3,2,0:T(2,128)S(1)}, u32[]{:S(2)}, u32[]{:S(2)}) collective-permute-start(s32[3,36,20,2]{1,3,2,0:T(2,128)} %copy.193), channel_id=1, source_target_pairs={{0,1},{2,3},{4,5},{6,7},{8,9},{10,11},{12,13},{14,15},{16,17},{18,... | collective-permute-start | bytes 51848 | tf_op jit(solution)/shard_map/ppermute | solution.py:19
  28.2 3.3 %collective-permute-start.5 = (s32[3,36,20,2]{1,3,2,0:T(2,128)S(1)}, s32[3,36,20,2]{1,3,2,0:T(2,128)}, u32[]{:S(2)}, u32[]{:S(2)}) collective-permute-start(s32[3,36,20,2]{1,3,2,0:T(2,128)S(1)} %copy.194), channel_id=1, source_target_pairs={{1,0},{3,2},{5,4},{7,6},{9,8},{11,10},{13,12},{15,14},{17,16},{19,... | collective-permute-start | bytes 51848 | tf_op jit(solution)/shard_map/ppermute | solution.py:21
  37.2 3.5 %copy-start.2 = (f32[36,20,132]{2,1,0:T(8,128)}, f32[36,20,132]{2,1,0:T(8,128)S(1)}, u32[]{:S(2)}) copy-start(f32[36,20,132]{2,1,0:T(8,128)S(1)} %convert_multiply_fusion) | copy-start | bytes 1140484
  40.6 5.7 %copy-start.3 = (f32[9,32,16,128]{3,2,1,0:T(8,128)S(1)}, f32[9,32,16,128]{3,2,1,0:T(8,128)}, u32[]{:S(2)}) copy-start(f32[9,32,16,128]{3,2,1,0:T(8,128)} %param.5) | copy-start | bytes 7077892
  46.5 38.1 %copy-start.1 = (f32[9,32,16,128]{3,2,1,0:T(8,128)}, f32[9,32,16,128]{3,2,1,0:T(8,128)S(1)}, u32[]{:S(2)}) copy-start(f32[9,32,16,128]{3,2,1,0:T(8,128)S(1)} %broadcast_multiply_fusion) | copy-start | bytes 7077892
  46.6 11.0 %collective-permute-start.6 = (f32[9,1,16,128]{3,2,1,0:T(8,128)S(1)}, f32[9,1,16,128]{3,2,1,0:T(8,128)S(1)}, u32[]{:S(2)}, u32[]{:S(2)}) collective-permute-start(f32[9,1,16,128]{3,2,1,0:T(8,128)S(1)} %get-tuple-element.30), channel_id=1, source_target_pairs={{0,8},{8,16},{16,24},{1,9},{9,17},{17,25},{2,10},{10,18},{18,26},{... | collective-permute-start | bytes 221192 | tf_op jit(solution)/shard_map/ppermute | solution.py:19
  50.9 6.7 %collective-permute-start.7 = (f32[9,1,16,128]{3,2,1,0:T(8,128)S(1)}, f32[9,1,16,128]{3,2,1,0:T(8,128)S(1)}, u32[]{:S(2)}, u32[]{:S(2)}) collective-permute-start(f32[9,1,16,128]{3,2,1,0:T(8,128)S(1)} %get-tuple-element.31), channel_id=1, source_target_pairs={{8,0},{16,8},{24,16},{9,1},{17,9},{25,17},{10,2},{18,10},{26,18},{... | collective-permute-start | bytes 221192 | tf_op jit(solution)/shard_map/ppermute | solution.py:21
  57.9 9.1 %collective-permute-start.9 = (f32[9,34,1,128]{3,1,2,0:T(8,128)S(1)}, f32[9,34,1,128]{3,1,2,0:T(8,128)S(1)}, u32[]{:S(2)}, u32[]{:S(2)}) collective-permute-start(f32[9,34,1,128]{3,1,2,0:T(8,128)S(1)} %copy.198), channel_id=1, source_target_pairs={{2,0},{4,2},{6,4},{3,1},{5,3},{7,5},{10,8},{12,10},{14,12},{11,9},... | collective-permute-start | bytes 470024 | tf_op jit(solution)/shard_map/ppermute | solution.py:21
  59.2 8.5 %collective-permute-start.8 = (f32[9,34,1,128]{3,1,2,0:T(8,128)S(1)}, f32[9,34,1,128]{3,1,2,0:T(8,128)S(1)}, u32[]{:S(2)}, u32[]{:S(2)}) collective-permute-start(f32[9,34,1,128]{3,1,2,0:T(8,128)S(1)} %copy.197), channel_id=1, source_target_pairs={{0,2},{2,4},{4,6},{1,3},{3,5},{5,7},{8,10},{10,12},{12,14},{9,11},... | collective-permute-start | bytes 470024 | tf_op jit(solution)/shard_map/ppermute | solution.py:19
  79.7 12.6 %collective-permute-start.11 = (f32[9,34,18,1]{1,2,3,0:T(8,128)S(1)}, f32[9,34,18,1]{1,2,3,0:T(8,128)S(1)}, u32[]{:S(2)}, u32[]{:S(2)}) collective-permute-start(f32[9,34,18,1]{1,2,3,0:T(8,128)S(1)} %copy.204), channel_id=1, source_target_pairs={{1,0},{3,2},{5,4},{7,6},{9,8},{11,10},{13,12},{15,14},{17,16},{19,... | collective-permute-start | bytes 66104 | tf_op jit(solution)/shard_map/ppermute | solution.py:21
  81.0 7.4 %collective-permute-start.10 = (f32[9,34,18,1]{1,2,3,0:T(8,128)S(1)}, f32[9,34,18,1]{1,2,3,0:T(8,128)}, u32[]{:S(2)}, u32[]{:S(2)}) collective-permute-start(f32[9,34,18,1]{1,2,3,0:T(8,128)S(1)} %copy.201), channel_id=1, source_target_pairs={{0,1},{2,3},{4,5},{6,7},{8,9},{10,11},{12,13},{14,15},{16,17},{18,... | collective-permute-start | bytes 66104 | tf_op jit(solution)/shard_map/ppermute | solution.py:19
  144.3 22.1 %copy-start = (f32[9,32,16,128]{3,2,1,0:T(8,128)S(1)}, f32[9,32,16,128]{3,2,1,0:T(8,128)}, u32[]{:S(2)}) copy-start(f32[9,32,16,128]{3,2,1,0:T(8,128)} %fusion.30) | copy-start | bytes 7077892
  144.3 6.4 %collective-permute-start.12 = (f32[9,1,16,128]{3,2,1,0:T(8,128)S(1)}, f32[9,1,16,128]{3,2,1,0:T(8,128)S(1)}, u32[]{:S(2)}, u32[]{:S(2)}) collective-permute-start(f32[9,1,16,128]{3,2,1,0:T(8,128)S(1)} %get-tuple-element.28), channel_id=1, source_target_pairs={{0,8},{8,16},{16,24},{1,9},{9,17},{17,25},{2,10},{10,18},{18,26},{... | collective-permute-start | bytes 221192 | tf_op jit(solution)/shard_map/ppermute | solution.py:19
  148.7 6.2 %collective-permute-start.13 = (f32[9,1,16,128]{3,2,1,0:T(8,128)S(1)}, f32[9,1,16,128]{3,2,1,0:T(8,128)S(1)}, u32[]{:S(2)}, u32[]{:S(2)}) collective-permute-start(f32[9,1,16,128]{3,2,1,0:T(8,128)S(1)} %get-tuple-element.29), channel_id=1, source_target_pairs={{8,0},{16,8},{24,16},{9,1},{17,9},{25,17},{10,2},{18,10},{26,18},{... | collective-permute-start | bytes 221192 | tf_op jit(solution)/shard_map/ppermute | solution.py:21
  156.9 8.6 %collective-permute-start.15 = (f32[9,34,1,128]{3,1,2,0:T(8,128)S(1)}, f32[9,34,1,128]{3,1,2,0:T(8,128)S(1)}, u32[]{:S(2)}, u32[]{:S(2)}) collective-permute-start(f32[9,34,1,128]{3,1,2,0:T(8,128)S(1)} %copy.208), channel_id=1, source_target_pairs={{2,0},{4,2},{6,4},{3,1},{5,3},{7,5},{10,8},{12,10},{14,12},{11,9},... | collective-permute-start | bytes 470024 | tf_op jit(solution)/shard_map/ppermute | solution.py:21
  158.2 8.1 %collective-permute-start.14 = (f32[9,34,1,128]{3,1,2,0:T(8,128)S(1)}, f32[9,34,1,128]{3,1,2,0:T(8,128)S(1)}, u32[]{:S(2)}, u32[]{:S(2)}) collective-permute-start(f32[9,34,1,128]{3,1,2,0:T(8,128)S(1)} %copy.207), channel_id=1, source_target_pairs={{0,2},{2,4},{4,6},{1,3},{3,5},{5,7},{8,10},{10,12},{12,14},{9,11},... | collective-permute-start | bytes 470024 | tf_op jit(solution)/shard_map/ppermute | solution.py:19
  178.5 10.4 %collective-permute-start.17 = (f32[9,34,18,1]{1,2,3,0:T(8,128)S(1)}, f32[9,34,18,1]{1,2,3,0:T(8,128)S(1)}, u32[]{:S(2)}, u32[]{:S(2)}) collective-permute-start(f32[9,34,18,1]{1,2,3,0:T(8,128)S(1)} %copy.214), channel_id=1, source_target_pairs={{0,1},{2,3},{4,5},{6,7},{8,9},{10,11},{12,13},{14,15},{16,17},{18,... | collective-permute-start | bytes 66104 | tf_op jit(solution)/shard_map/ppermute | solution.py:19
  179.8 5.1 %collective-permute-start.16 = (f32[9,34,18,1]{1,2,3,0:T(8,128)S(1)}, f32[9,34,18,1]{1,2,3,0:T(8,128)}, u32[]{:S(2)}, u32[]{:S(2)}) collective-permute-start(f32[9,34,18,1]{1,2,3,0:T(8,128)S(1)} %copy.211), channel_id=1, source_target_pairs={{1,0},{3,2},{5,4},{7,6},{9,8},{11,10},{13,12},{15,14},{17,16},{19,... | collective-permute-start | bytes 66104 | tf_op jit(solution)/shard_map/ppermute | solution.py:21
where the time goes:
time: 278 us; the launch traced here: 277 us
  other arithmetic  124 us (45%)
  local copies, waits for them, and re-layouts  45.8 us (16%)
  starting transfers between devices  44.9 us (16%)
  blocking collectives  43 us (15%)
  waiting for transfers between devices  17.5 us (6%)
    psum x1, blocking collectives, per_device(): lax.psum(local_sums, ('gx', 'gy', 'gz')) / math.sqrt(cell_count)  43 us
    div x1, other arithmetic, per_device(): quotas = amounts / (gathered + beyond)  36.9 us
    concatenate x8, other arithmetic, padded(): jnp.concatenate([lax.ppermute(tail, axis, [(i, (i + 1) % count) for i in...  35.3 us
    ppermute x9, starting transfers between devices, padded(): lax.ppermute(tail, axis, [(i, (i + 1) % count) for i in range(ends)])  33.3 us
    reduce_sum x1, other arithmetic, per_device(): local_sums = jnp.sum(volume_mid[None] * redistributed, axis=(1, 2, 3))  29.8 us
    ppermute x9, waiting for transfers between devices, padded(): lax.ppermute(head, axis, [((i + 1) % count, i) for i in range(ends)])  14.2 us
    slice x9, local copies, waits for them, and re-layouts, padded(): lax.slice_in_dim(cells, cells.shape[dim] - width, cells.shape[dim], axis=...  13.8 us
    slice x6, local copies, waits for them, and re-layouts, padded(): head = lax.slice_in_dim(cells, 0, width, axis=dim)  12 us
  transfers between devices with their start and end apart: 18, of which 9 were waited for; matrix products, arithmetic and copies ran while one was open for 10% of the time, Pallas kernels for 0%

commit v1 on v0

--- a/solution.py
+++ b/solution.py
@@ -98,7 +98,7 @@
         * lax.axis_size("gz")
     )
     local_sums = jnp.sum(volume_mid[None] * redistributed, axis=(1, 2, 3))
-    species_change = lax.psum(local_sums, ("gx", "gy", "gz")) / math.sqrt(cell_count)
+    species_change = lax.psum(lax.psum(local_sums, ("gy", "gz")), "gx") / math.sqrt(cell_count)
     return (redistributed, species_change)
 
 

time: 278 us -> 263 us (0.946)
  blocking collectives: 43 us -> 29.7 us
    psum x1 -> x2, blocking collectives: 43 us -> 29.7 us  [the longest x1 19.9 us: per_device(): lax.psum(local_sums, ('gy', 'gz'))]
where the time goes in v1:
time: 263 us; the launch traced here: 262 us
  other arithmetic  123 us (47%)
  local copies, waits for them, and re-layouts  45.8 us (17%)
  starting transfers between devices  44.9 us (17%)
  blocking collectives  29.7 us (11%)
  waiting for transfers between devices  17.5 us (7%)
    div x1, other arithmetic, per_device(): quotas = amounts / (gathered + beyond)  36.5 us
    concatenate x8, other arithmetic, padded(): jnp.concatenate([lax.ppermute(tail, axis, [(i, (i + 1) % count) for i in...  35.2 us
    ppermute x9, starting transfers between devices, padded(): lax.ppermute(tail, axis, [(i, (i + 1) % count) for i in range(ends)])  33.3 us
    reduce_sum x1, other arithmetic, per_device(): local_sums = jnp.sum(volume_mid[None] * redistributed, axis=(1, 2, 3))  29.3 us
    psum x1, blocking collectives, per_device(): lax.psum(local_sums, ('gy', 'gz'))  19.9 us
    ppermute x9, waiting for transfers between devices, padded(): lax.ppermute(head, axis, [((i + 1) % count, i) for i in range(ends)])  14.2 us
    slice x9, local copies, waits for them, and re-layouts, padded(): lax.slice_in_dim(cells, cells.shape[dim] - width, cells.shape[dim], axis=...  13.8 us
    slice x6, local copies, waits for them, and re-layouts, padded(): head = lax.slice_in_dim(cells, 0, width, axis=dim)  12 us
  transfers between devices with their start and end apart: 18, of which 9 were waited for; matrix products, arithmetic and copies ran while one was open for 10% of the time, Pallas kernels for 0%

profile of v1, /device:TPU:0, one launch (start us, length us, event | category | flops | bytes accessed | tf_op | source)
XLA Modules:
  0.0 262.4 jit_solution(8665359106191824397)
XLA Ops:
  0.6 1.1 select_bitcast_fusion.2
  1.7 1.1 select_bitcast_fusion.1
  2.8 4.9 %collective-permute-start = (s32[3,2,16,128]{3,2,1,0:T(8,128)S(1)}, s32[3,2,16,128]{3,2,1,0:T(8,128)S(1)}, u32[]{:S(2)}, u32[]{:S(2)}) collective-permute-start(s32[3,2,16,128]{3,2,1,0:T(8,128)S(1)} %get-tuple-element.91), channel_id=1, source_target_pairs={{0,8},{8,16},{16,24},{1,9},{9,17},{17,25},{2,10},{10,18},{18,26},{... | collective-permute-start | bytes 147464 | tf_op jit(solution)/shard_map/ppermute | solution.py:19
  7.7 1.3 collective-permute-start.1
  9.4 4.2 %collective-permute-done.1 = s32[3,2,16,128]{3,2,1,0:T(8,128)S(1)} collective-permute-done((s32[3,2,16,128]{3,2,1,0:T(8,128)S(1)}, s32[3,2,16,128]{3,2,1,0:T(8,128)S(1)}, u32[]{:S(2)}, u32[]{:S(2)}) %collective-permute-start.1) | collective-permute-done | bytes 49184 | tf_op jit(solution)/shard_map/ppermute | solution.py:21
  13.8 3.5 %collective-permute-start.2 = (s32[3,36,2,128]{3,2,1,0:T(2,128)S(1)}, s32[3,36,2,128]{3,2,1,0:T(2,128)S(1)}, u32[]{:S(2)}, u32[]{:S(2)}) collective-permute-start(s32[3,36,2,128]{3,2,1,0:T(2,128)S(1)} %get-tuple-element.87), channel_id=1, source_target_pairs={{0,2},{2,4},{4,6},{1,3},{3,5},{5,7},{8,10},{10,12},{12,14},{9,11},... | collective-permute-start | bytes 331784 | tf_op jit(solution)/shard_map/ppermute | solution.py:19
  17.3 1.3 collective-permute-start.3
  18.6 1.0 collective-permute-done.2
  19.6 4.3 %collective-permute-done.3 = s32[3,36,2,128]{3,2,1,0:T(2,128)S(1)} collective-permute-done((s32[3,36,2,128]{3,2,1,0:T(2,128)S(1)}, s32[3,36,2,128]{3,2,1,0:T(2,128)S(1)}, u32[]{:S(2)}, u32[]{:S(2)}) %collective-permute-start.3) | collective-permute-done | bytes 110624 | tf_op jit(solution)/shard_map/ppermute | solution.py:21
  23.9 0.6 copy-done.4
  25.2 1.2 copy.193
  26.3 1.3 collective-permute-start.4
  27.6 0.5 copy.194
  28.2 1.3 collective-permute-start.5
  29.5 0.6 copy.195
  30.1 1.3 collective-permute-done.5
  31.4 1.5 copy.196
  32.9 4.2 %pad_add_fusion = s32[3,36,20,132]{3,2,1,0:T(8,128)S(1)} fusion(s32[3,36,20,2]{3,2,1,0:T(8,128)S(1)} %copy.196, s32[3,36,2,128]{3,2,1,0:T(2,128)} %copy-done.4, s32[3,2,16,128]{3,2,1,0:T(8,128)} %copy-done.6, s32[1,32,16,128]{3,2,1,0:T(8,128)S(1)} %get-tuple-element.94, s32[1,32,16,128]{3,2,1,0:T(8,128)S(1)} %get-tuple-element.93, ...), kind=kLoop, calls=%fused_computation.10 | loop fusion | flops 2280960 | bytes 2280960 | tf_op jit(solution)/shard_map/concatenate | solution.py:17
  37.7 3.0 %fusion.220 = (f32[32,16,128]{2,1,0:T(8,128)}, f32[32,16,128]{2,1,0:T(8,128)}, f32[32,16,128]{2,1,0:T(8,128)}, f32[32,16,128]{2,1,0:T(8,128)}, f32[32,16,128]{2,...) fusion(s32[36,20,132]{2,1,0:T(8,128)S(1)} %get-tuple-element.19), kind=kLoop, calls=%fused_computation.373 | loop fusion | flops 3735552 | bytes 5505024 | tf_op jit(solution)/shard_map/convert_element_type | solution.py:44
  40.6 4.8 %fusion.61 = (f32[34,18,130]{2,1,0:T(8,128)S(1)}, f32[34,18,130]{2,1,0:T(8,128)S(1)}) fusion(f32[36,20,132]{2,1,0:T(8,128)S(1)} %fusion.60, f32[36,20,132]{2,1,0:T(8,128)S(1)} %convert_multiply_fusion, s32[36,20,132]{2,1,0:T(8,128)S(1)} %get-tuple-element.19), kind=kLoop, calls=%fused_computation.132 | loop fusion | flops 8672040 | bytes 9865440 | tf_op jit(solution)/shard_map/div | solution.py:68
  45.4 1.0 slice_divide_fusion.1
  46.6 4.3 %collective-permute-start.6 = (f32[9,1,16,128]{3,2,1,0:T(8,128)S(1)}, f32[9,1,16,128]{3,2,1,0:T(8,128)S(1)}, u32[]{:S(2)}, u32[]{:S(2)}) collective-permute-start(f32[9,1,16,128]{3,2,1,0:T(8,128)S(1)} %get-tuple-element.30), channel_id=1, source_target_pairs={{0,8},{8,16},{16,24},{1,9},{9,17},{17,25},{2,10},{10,18},{18,26},{... | collective-permute-start | bytes 221192 | tf_op jit(solution)/shard_map/ppermute | solution.py:19
  50.9 1.3 collective-permute-start.7
  52.2 2.3 fusion.193
  54.5 3.1 %fusion.191 = (f32[32,16,128]{2,1,0:T(8,128)}, f32[32,16,128]{2,1,0:T(8,128)}, f32[32,16,128]{2,1,0:T(8,128)}, f32[32,16,128]{2,1,0:T(8,128)}, f32[32,16,128]{2,...) fusion(s32[36,20,132]{2,1,0:T(8,128)S(1)} %get-tuple-element.19), kind=kLoop, calls=%fused_computation.314 | loop fusion | flops 3735552 | bytes 8126464 | tf_op jit(solution)/shard_map/convert_element_type | solution.py:44
  57.9 1.3 collective-permute-start.9
  59.2 4.7 %collective-permute-start.8 = (f32[9,34,1,128]{3,1,2,0:T(8,128)S(1)}, f32[9,34,1,128]{3,1,2,0:T(8,128)S(1)}, u32[]{:S(2)}, u32[]{:S(2)}) collective-permute-start(f32[9,34,1,128]{3,1,2,0:T(8,128)S(1)} %copy.197), channel_id=1, source_target_pairs={{0,2},{2,4},{4,6},{1,3},{3,5},{5,7},{8,10},{10,12},{12,14},{9,11},... | collective-permute-start | bytes 470024 | tf_op jit(solution)/shard_map/ppermute | solution.py:19
  63.9 3.0 %fusion.189 = (f32[32,16,128]{2,1,0:T(8,128)}, f32[32,16,128]{2,1,0:T(8,128)}, f32[32,16,128]{2,1,0:T(8,128)}, f32[32,16,128]{2,1,0:T(8,128)}, f32[32,16,128]{2,...) fusion(s32[36,20,132]{2,1,0:T(8,128)S(1)} %get-tuple-element.19), kind=kLoop, calls=%fused_computation.311 | loop fusion | flops 2949120 | bytes 7864320 | tf_op jit(solution)/shard_map/convert_element_type | solution.py:44
  67.1 0.5 collective-permute-done.8
  67.8 0.6 pad_maximum_fusion.2
  68.5 4.2 %fusion.224 = (f32[9,34,18,1]{3,2,1,0:T(8,128)}, f32[9,34,18,1]{3,2,1,0:T(8,128)}) fusion(f32[9,34,18,128]{3,2,1,0:T(8,128)S(1)} %pad_maximum_fusion.2), kind=kLoop, calls=%fused_computation.422 | loop fusion | bytes 88128 | tf_op jit(solution)/shard_map/slice | solution.py:16
  72.6 3.5 %copy.201 = f32[9,34,18,1]{1,2,3,0:T(8,128)S(1)} copy(f32[9,34,18,1]{3,2,1,0:T(8,128)} %get-tuple-element.12) | data formatting | bytes 44064 | tf_op jit(solution)/shard_map/slice | solution.py:16
  76.2 3.5 %copy.204 = f32[9,34,18,1]{1,2,3,0:T(8,128)S(1)} copy(f32[9,34,18,1]{3,2,1,0:T(8,128)} %get-tuple-element.13) | data formatting | bytes 44064 | tf_op jit(solution)/shard_map/slice | solution.py:15
  79.7 1.3 collective-permute-start.11
  81.0 3.7 %collective-permute-start.10 = (f32[9,34,18,1]{1,2,3,0:T(8,128)S(1)}, f32[9,34,18,1]{1,2,3,0:T(8,128)}, u32[]{:S(2)}, u32[]{:S(2)}) collective-permute-start(f32[9,34,18,1]{1,2,3,0:T(8,128)S(1)} %copy.201), channel_id=1, source_target_pairs={{0,1},{2,3},{4,5},{6,7},{8,9},{10,11},{12,13},{14,15},{16,17},{18,... | collective-permute-start | bytes 66104 | tf_op jit(solution)/shard_map/ppermute | solution.py:19
  84.7 3.8 %maximum_maximum_fusion.2 = (f32[9,34,17,128]{3,2,1,0:T(8,128)}, f32[9,34,17,128]{3,2,1,0:T(8,128)}) fusion(f32[9,1,16,128]{3,2,1,0:T(8,128)S(1)} %collective-permute-done.7, f32[9,32,16,128]{3,2,1,0:T(8,128)S(1)} %broadcast_multiply_fusion, f32[9,1,16,128]{3,2,1,0:T(8,128)S(1)} %collective-permute-done.6, f32[9,34,1,128]{3,2,1,0:T(1,128)S(1)} %copy.199, ...), kind=kLoop, calls=%fused_computation.5 | loop fusion | flops 3995136 | bytes 8146944 | tf_op jit(solution)/shard_map/concatenate | solution.py:17
  88.5 3.9 %copy.202 = f32[9,34,18,1]{3,2,1,0:T(8,128)} copy(f32[9,34,18,1]{1,2,3,0:T(8,128)} %collective-permute-done.10) | data formatting | bytes 44064 | tf_op jit(solution)/shard_map/ppermute | solution.py:19
  92.4 3.2 %copy.205 = f32[9,34,18,1]{3,2,1,0:T(8,128)} copy(f32[9,34,18,1]{1,2,3,0:T(8,128)S(1)} %collective-permute-done.11) | data formatting | bytes 44064 | tf_op jit(solution)/shard_map/ppermute | solution.py:21
  95.6 10.9 %maximum_maximum_fusion = (f32[9,34,18,129]{3,2,1,0:T(8,128)S(1)}, f32[9,34,18,129]{3,2,1,0:T(8,128)}) fusion(f32[9,34,1,128]{3,2,1,0:T(1,128)S(1)} %copy.200, f32[9,1,16,128]{3,2,1,0:T(8,128)S(1)} %collective-permute-done.7, f32[9,32,16,128]{3,2,1,0:T(8,128)} %copy-done.1, f32[9,1,16,128]{3,2,1,0:T(8,128)S(1)} %collective-permute-done.6, ...), kind=kLoop, calls=%fused_computation | loop fusion | flops 7105320 | bytes 8548416 | tf_op jit(solution)/shard_map/concatenate | solution.py:17
  106.5 36.5 %fusion.30 = f32[9,32,16,128]{3,2,1,0:T(8,128)} fusion(f32[9,34,18,129]{3,2,1,0:T(8,128)} %get-tuple-element.17, f32[9,34,17,128]{3,2,1,0:T(8,128)} %get-tuple-element.25, f32[9,34,18,129]{3,2,1,0:T(8,128)S(1)} %get-tuple-element.16, f32[9,1,16,128]{3,2,1,0:T(8,128)S(1)} %collective-permute-done.7, f32[9,32,16,128]{3,2,1,0:T(8,128)} %copy-done.1, ...), kind=kLoop, calls=%fused_computation.68 | loop fusion | flops 33030144 | bytes 68829184 | tf_op jit(solution)/shard_map/div | solution.py:84
  143.0 0.9 fusion.225
  144.0 4.4 %collective-permute-start.12 = (f32[9,1,16,128]{3,2,1,0:T(8,128)S(1)}, f32[9,1,16,128]{3,2,1,0:T(8,128)S(1)}, u32[]{:S(2)}, u32[]{:S(2)}) collective-permute-start(f32[9,1,16,128]{3,2,1,0:T(8,128)S(1)} %get-tuple-element.28), channel_id=1, source_target_pairs={{0,8},{8,16},{16,24},{1,9},{9,17},{17,25},{2,10},{10,18},{18,26},{... | collective-permute-start | bytes 221192 | tf_op jit(solution)/shard_map/ppermute | solution.py:19
  148.4 1.3 collective-permute-start.13
  149.7 0.7 collective-permute-done.12
  150.4 4.3 %collective-permute-done.13 = f32[9,1,16,128]{3,2,1,0:T(8,128)S(1)} collective-permute-done((f32[9,1,16,128]{3,2,1,0:T(8,128)S(1)}, f32[9,1,16,128]{3,2,1,0:T(8,128)S(1)}, u32[]{:S(2)}, u32[]{:S(2)}) %collective-permute-start.13) | collective-permute-done | bytes 73760 | tf_op jit(solution)/shard_map/ppermute | solution.py:21
  154.6 1.9 pad_maximum_fusion.12
  156.6 1.3 collective-permute-start.15
  157.9 5.2 %collective-permute-start.14 = (f32[9,34,1,128]{3,1,2,0:T(8,128)S(1)}, f32[9,34,1,128]{3,1,2,0:T(8,128)S(1)}, u32[]{:S(2)}, u32[]{:S(2)}) collective-permute-start(f32[9,34,1,128]{3,1,2,0:T(8,128)S(1)} %copy.207), channel_id=1, source_target_pairs={{0,2},{2,4},{4,6},{1,3},{3,5},{5,7},{8,10},{10,12},{12,14},{9,11},... | collective-permute-start | bytes 470024 | tf_op jit(solution)/shard_map/ppermute | solution.py:19
  163.1 2.0 slice.847
  165.3 0.7 collective-permute-done.14
  166.1 0.6 pad_maximum_fusion.4
  166.7 4.3 %fusion.223 = (f32[9,34,18,1]{3,2,1,0:T(8,128)}, f32[9,34,18,1]{3,2,1,0:T(8,128)}) fusion(f32[9,34,18,128]{3,2,1,0:T(8,128)S(1)} %pad_maximum_fusion.4), kind=kLoop, calls=%fused_computation.421 | loop fusion | bytes 88128 | tf_op jit(solution)/shard_map/slice | solution.py:15
  171.1 3.5 %copy.211 = f32[9,34,18,1]{1,2,3,0:T(8,128)S(1)} copy(f32[9,34,18,1]{3,2,1,0:T(8,128)} %get-tuple-element.10) | data formatting | bytes 44064 | tf_op jit(solution)/shard_map/slice | solution.py:15
  174.6 3.5 %copy.214 = f32[9,34,18,1]{1,2,3,0:T(8,128)S(1)} copy(f32[9,34,18,1]{3,2,1,0:T(8,128)} %get-tuple-element.11) | data formatting | bytes 44064 | tf_op jit(solution)/shard_map/slice | solution.py:16
  178.2 1.3 collective-permute-start.17
  179.5 1.3 collective-permute-start.16
  180.8 3.8 %pad_maximum_fusion.5 = (f32[9,34,17,128]{3,2,1,0:T(8,128)}, f32[9,34,17,128]{3,2,1,0:T(8,128)}) fusion(f32[9,34,1,128]{3,2,1,0:T(1,128)S(1)} %copy.210, f32[9,1,16,128]{3,2,1,0:T(8,128)S(1)} %collective-permute-done.13, f32[9,32,16,128]{3,2,1,0:T(8,128)S(1)} %copy-done, f32[9,1,16,128]{3,2,1,0:T(8,128)S(1)} %collective-permute-done.12, ...), kind=kLoop, calls=%fused_computation.8 | loop fusion | flops 3995136 | bytes 8146944 | tf_op jit(solution)/shard_map/concatenate | solution.py:17
  184.6 4.0 %copy.212 = f32[9,34,18,1]{3,2,1,0:T(8,128)} copy(f32[9,34,18,1]{1,2,3,0:T(8,128)} %collective-permute-done.16) | data formatting | bytes 44064 | tf_op jit(solution)/shard_map/ppermute | solution.py:21
  188.6 3.2 %copy.215 = f32[9,34,18,1]{3,2,1,0:T(8,128)} copy(f32[9,34,18,1]{1,2,3,0:T(8,128)S(1)} %collective-permute-done.17) | data formatting | bytes 44064 | tf_op jit(solution)/shard_map/ppermute | solution.py:19
  191.8 11.0 %pad_maximum_fusion.1 = (f32[9,34,18,129]{3,2,1,0:T(8,128)S(1)}, f32[9,34,18,129]{3,2,1,0:T(8,128)}) fusion(f32[9,34,18,1]{3,2,1,0:T(8,128)} %copy.212, f32[9,34,1,128]{3,2,1,0:T(1,128)S(1)} %copy.210, f32[9,1,16,128]{3,2,1,0:T(8,128)S(1)} %collective-permute-done.13, f32[9,32,16,128]{3,2,1,0:T(8,128)} %fusion.30, ...), kind=kLoop, calls=%fused_computation.2 | loop fusion | flops 7105320 | bytes 8548416 | tf_op jit(solution)/shard_map/concatenate | solution.py:17
  202.8 29.3 %multiply_reduce_fusion = (f32[9]{0:T(128)S(1)}, f32[9,32,16,128]{3,2,1,0:T(8,128)}) fusion(f32[32,16,128]{2,1,0:T(8,128)} %slice.847, f32[9,34,18,129]{3,2,1,0:T(8,128)} %get-tuple-element.15, f32[32,16,128]{2,1,0:T(8,128)} %get-tuple-element.62, f32[9,34,17,128]{3,2,1,0:T(8,128)} %get-tuple-element.21, f32[32,16,128]{2,1,0:T(8,128)} %get-tuple-element.63, ...), kind=kLoop, calls=%fused_computation.121 | loop fusion | flops 34209784 | bytes 69091360 | tf_op jit(solution)/shard_map/reduce_sum | solution.py:100
  232.1 19.9 %psum.14 = f32[9]{0:T(128)S(1)} all-reduce(f32[9]{0:T(128)S(1)} %get-tuple-element.4), channel_id=1, replica_groups=mesh['gx'=4,'gy'=4,'gz'=2] {'gy','gz'}, use_global_device_ids=true, to_apply=%region_1.2 | all-reduce | flops 9 | bytes 72 | tf_op jit(solution)/shard_map/psum | solution.py:101
  252.0 9.8 %psum.15 = f32[9]{0:T(128)S(1)} all-reduce(f32[9]{0:T(128)S(1)} %psum.14), channel_id=1, replica_groups=mesh['gx'=4,'gy'=4,'gz'=2] {'gx'}, use_global_device_ids=true, to_apply=%region_2.3 | all-reduce | flops 9 | bytes 72 | tf_op jit(solution)/shard_map/psum | solution.py:101
  261.9 0.5 broadcast_multiply_fusion.1
  (42 shorter events, 2.8 us)
Async XLA Ops:
  2.8 6.6 %collective-permute-start = (s32[3,2,16,128]{3,2,1,0:T(8,128)S(1)}, s32[3,2,16,128]{3,2,1,0:T(8,128)S(1)}, u32[]{:S(2)}, u32[]{:S(2)}) collective-permute-start(s32[3,2,16,128]{3,2,1,0:T(8,128)S(1)} %get-tuple-element.91), channel_id=1, source_target_pairs={{0,8},{8,16},{16,24},{1,9},{9,17},{17,25},{2,10},{10,18},{18,26},{... | collective-permute-start | bytes 147464 | tf_op jit(solution)/shard_map/ppermute | solution.py:19
  7.7 6.0 %collective-permute-start.1 = (s32[3,2,16,128]{3,2,1,0:T(8,128)S(1)}, s32[3,2,16,128]{3,2,1,0:T(8,128)S(1)}, u32[]{:S(2)}, u32[]{:S(2)}) collective-permute-start(s32[3,2,16,128]{3,2,1,0:T(8,128)S(1)} %get-tuple-element.92), channel_id=1, source_target_pairs={{8,0},{16,8},{24,16},{9,1},{17,9},{25,17},{10,2},{18,10},{26,18},{... | collective-permute-start | bytes 147464 | tf_op jit(solution)/shard_map/ppermute | solution.py:21
  9.4 14.5 %copy-start.5 = (s32[3,2,16,128]{3,2,1,0:T(8,128)}, s32[3,2,16,128]{3,2,1,0:T(8,128)S(1)}, u32[]{:S(2)}) copy-start(s32[3,2,16,128]{3,2,1,0:T(8,128)S(1)} %collective-permute-done) | copy-start | bytes 147460
  13.7 10.2 %copy-start.6 = (s32[3,2,16,128]{3,2,1,0:T(8,128)}, s32[3,2,16,128]{3,2,1,0:T(8,128)S(1)}, u32[]{:S(2)}) copy-start(s32[3,2,16,128]{3,2,1,0:T(8,128)S(1)} %collective-permute-done.1) | copy-start | bytes 147460
  13.8 5.8 %collective-permute-start.2 = (s32[3,36,2,128]{3,2,1,0:T(2,128)S(1)}, s32[3,36,2,128]{3,2,1,0:T(2,128)S(1)}, u32[]{:S(2)}, u32[]{:S(2)}) collective-permute-start(s32[3,36,2,128]{3,2,1,0:T(2,128)S(1)} %get-tuple-element.87), channel_id=1, source_target_pairs={{0,2},{2,4},{4,6},{1,3},{3,5},{5,7},{8,10},{10,12},{12,14},{9,11},... | collective-permute-start | bytes 331784 | tf_op jit(solution)/shard_map/ppermute | solution.py:19
  17.3 6.6 %collective-permute-start.3 = (s32[3,36,2,128]{3,2,1,0:T(2,128)S(1)}, s32[3,36,2,128]{3,2,1,0:T(2,128)S(1)}, u32[]{:S(2)}, u32[]{:S(2)}) collective-permute-start(s32[3,36,2,128]{3,2,1,0:T(2,128)S(1)} %get-tuple-element.88), channel_id=1, source_target_pairs={{2,0},{4,2},{6,4},{3,1},{5,3},{7,5},{10,8},{12,10},{14,12},{11,9},... | collective-permute-start | bytes 331784 | tf_op jit(solution)/shard_map/ppermute | solution.py:21
  23.9 0.6 copy-start.4
  26.3 3.1 %collective-permute-start.4 = (s32[3,36,20,2]{1,3,2,0:T(2,128)}, s32[3,36,20,2]{1,3,2,0:T(2,128)S(1)}, u32[]{:S(2)}, u32[]{:S(2)}) collective-permute-start(s32[3,36,20,2]{1,3,2,0:T(2,128)} %copy.193), channel_id=1, source_target_pairs={{0,1},{2,3},{4,5},{6,7},{8,9},{10,11},{12,13},{14,15},{16,17},{18,... | collective-permute-start | bytes 51848 | tf_op jit(solution)/shard_map/ppermute | solution.py:19
  28.2 3.3 %collective-permute-start.5 = (s32[3,36,20,2]{1,3,2,0:T(2,128)S(1)}, s32[3,36,20,2]{1,3,2,0:T(2,128)}, u32[]{:S(2)}, u32[]{:S(2)}) collective-permute-start(s32[3,36,20,2]{1,3,2,0:T(2,128)S(1)} %copy.194), channel_id=1, source_target_pairs={{1,0},{3,2},{5,4},{7,6},{9,8},{11,10},{13,12},{15,14},{17,16},{19,... | collective-permute-start | bytes 51848 | tf_op jit(solution)/shard_map/ppermute | solution.py:21
  37.2 3.5 %copy-start.2 = (f32[36,20,132]{2,1,0:T(8,128)}, f32[36,20,132]{2,1,0:T(8,128)S(1)}, u32[]{:S(2)}) copy-start(f32[36,20,132]{2,1,0:T(8,128)S(1)} %convert_multiply_fusion) | copy-start | bytes 1140484
  40.6 5.7 %copy-start.3 = (f32[9,32,16,128]{3,2,1,0:T(8,128)S(1)}, f32[9,32,16,128]{3,2,1,0:T(8,128)}, u32[]{:S(2)}) copy-start(f32[9,32,16,128]{3,2,1,0:T(8,128)} %param.5) | copy-start | bytes 7077892
  46.6 38.2 %copy-start.1 = (f32[9,32,16,128]{3,2,1,0:T(8,128)}, f32[9,32,16,128]{3,2,1,0:T(8,128)S(1)}, u32[]{:S(2)}) copy-start(f32[9,32,16,128]{3,2,1,0:T(8,128)S(1)} %broadcast_multiply_fusion) | copy-start | bytes 7077892
  46.6 11.0 %collective-permute-start.6 = (f32[9,1,16,128]{3,2,1,0:T(8,128)S(1)}, f32[9,1,16,128]{3,2,1,0:T(8,128)S(1)}, u32[]{:S(2)}, u32[]{:S(2)}) collective-permute-start(f32[9,1,16,128]{3,2,1,0:T(8,128)S(1)} %get-tuple-element.30), channel_id=1, source_target_pairs={{0,8},{8,16},{16,24},{1,9},{9,17},{17,25},{2,10},{10,18},{18,26},{... | collective-permute-start | bytes 221192 | tf_op jit(solution)/shard_map/ppermute | solution.py:19
  50.9 6.7 %collective-permute-start.7 = (f32[9,1,16,128]{3,2,1,0:T(8,128)S(1)}, f32[9,1,16,128]{3,2,1,0:T(8,128)S(1)}, u32[]{:S(2)}, u32[]{:S(2)}) collective-permute-start(f32[9,1,16,128]{3,2,1,0:T(8,128)S(1)} %get-tuple-element.31), channel_id=1, source_target_pairs={{8,0},{16,8},{24,16},{9,1},{17,9},{25,17},{10,2},{18,10},{26,18},{... | collective-permute-start | bytes 221192 | tf_op jit(solution)/shard_map/ppermute | solution.py:21
  57.9 9.1 %collective-permute-start.9 = (f32[9,34,1,128]{3,1,2,0:T(8,128)S(1)}, f32[9,34,1,128]{3,1,2,0:T(8,128)S(1)}, u32[]{:S(2)}, u32[]{:S(2)}) collective-permute-start(f32[9,34,1,128]{3,1,2,0:T(8,128)S(1)} %copy.198), channel_id=1, source_target_pairs={{2,0},{4,2},{6,4},{3,1},{5,3},{7,5},{10,8},{12,10},{14,12},{11,9},... | collective-permute-start | bytes 470024 | tf_op jit(solution)/shard_map/ppermute | solution.py:21
  59.2 8.5 %collective-permute-start.8 = (f32[9,34,1,128]{3,1,2,0:T(8,128)S(1)}, f32[9,34,1,128]{3,1,2,0:T(8,128)S(1)}, u32[]{:S(2)}, u32[]{:S(2)}) collective-permute-start(f32[9,34,1,128]{3,1,2,0:T(8,128)S(1)} %copy.197), channel_id=1, source_target_pairs={{0,2},{2,4},{4,6},{1,3},{3,5},{5,7},{8,10},{10,12},{12,14},{9,11},... | collective-permute-start | bytes 470024 | tf_op jit(solution)/shard_map/ppermute | solution.py:19
  79.7 12.7 %collective-permute-start.11 = (f32[9,34,18,1]{1,2,3,0:T(8,128)S(1)}, f32[9,34,18,1]{1,2,3,0:T(8,128)S(1)}, u32[]{:S(2)}, u32[]{:S(2)}) collective-permute-start(f32[9,34,18,1]{1,2,3,0:T(8,128)S(1)} %copy.204), channel_id=1, source_target_pairs={{1,0},{3,2},{5,4},{7,6},{9,8},{11,10},{13,12},{15,14},{17,16},{19,... | collective-permute-start | bytes 66104 | tf_op jit(solution)/shard_map/ppermute | solution.py:21
  81.0 7.5 %collective-permute-start.10 = (f32[9,34,18,1]{1,2,3,0:T(8,128)S(1)}, f32[9,34,18,1]{1,2,3,0:T(8,128)}, u32[]{:S(2)}, u32[]{:S(2)}) collective-permute-start(f32[9,34,18,1]{1,2,3,0:T(8,128)S(1)} %copy.201), channel_id=1, source_target_pairs={{0,1},{2,3},{4,5},{6,7},{8,9},{10,11},{12,13},{14,15},{16,17},{18,... | collective-permute-start | bytes 66104 | tf_op jit(solution)/shard_map/ppermute | solution.py:19
  144.0 22.1 %copy-start = (f32[9,32,16,128]{3,2,1,0:T(8,128)S(1)}, f32[9,32,16,128]{3,2,1,0:T(8,128)}, u32[]{:S(2)}) copy-start(f32[9,32,16,128]{3,2,1,0:T(8,128)} %fusion.30) | copy-start | bytes 7077892
  144.0 6.4 %collective-permute-start.12 = (f32[9,1,16,128]{3,2,1,0:T(8,128)S(1)}, f32[9,1,16,128]{3,2,1,0:T(8,128)S(1)}, u32[]{:S(2)}, u32[]{:S(2)}) collective-permute-start(f32[9,1,16,128]{3,2,1,0:T(8,128)S(1)} %get-tuple-element.28), channel_id=1, source_target_pairs={{0,8},{8,16},{16,24},{1,9},{9,17},{17,25},{2,10},{10,18},{18,26},{... | collective-permute-start | bytes 221192 | tf_op jit(solution)/shard_map/ppermute | solution.py:19
  148.4 6.2 %collective-permute-start.13 = (f32[9,1,16,128]{3,2,1,0:T(8,128)S(1)}, f32[9,1,16,128]{3,2,1,0:T(8,128)S(1)}, u32[]{:S(2)}, u32[]{:S(2)}) collective-permute-start(f32[9,1,16,128]{3,2,1,0:T(8,128)S(1)} %get-tuple-element.29), channel_id=1, source_target_pairs={{8,0},{16,8},{24,16},{9,1},{17,9},{25,17},{10,2},{18,10},{26,18},{... | collective-permute-start | bytes 221192 | tf_op jit(solution)/shard_map/ppermute | solution.py:21
  156.6 8.6 %collective-permute-start.15 = (f32[9,34,1,128]{3,1,2,0:T(8,128)S(1)}, f32[9,34,1,128]{3,1,2,0:T(8,128)S(1)}, u32[]{:S(2)}, u32[]{:S(2)}) collective-permute-start(f32[9,34,1,128]{3,1,2,0:T(8,128)S(1)} %copy.208), channel_id=1, source_target_pairs={{2,0},{4,2},{6,4},{3,1},{5,3},{7,5},{10,8},{12,10},{14,12},{11,9},... | collective-permute-start | bytes 470024 | tf_op jit(solution)/shard_map/ppermute | solution.py:21
  157.9 8.1 %collective-permute-start.14 = (f32[9,34,1,128]{3,1,2,0:T(8,128)S(1)}, f32[9,34,1,128]{3,1,2,0:T(8,128)S(1)}, u32[]{:S(2)}, u32[]{:S(2)}) collective-permute-start(f32[9,34,1,128]{3,1,2,0:T(8,128)S(1)} %copy.207), channel_id=1, source_target_pairs={{0,2},{2,4},{4,6},{1,3},{3,5},{5,7},{8,10},{10,12},{12,14},{9,11},... | collective-permute-start | bytes 470024 | tf_op jit(solution)/shard_map/ppermute | solution.py:19
  178.2 10.4 %collective-permute-start.17 = (f32[9,34,18,1]{1,2,3,0:T(8,128)S(1)}, f32[9,34,18,1]{1,2,3,0:T(8,128)S(1)}, u32[]{:S(2)}, u32[]{:S(2)}) collective-permute-start(f32[9,34,18,1]{1,2,3,0:T(8,128)S(1)} %copy.214), channel_id=1, source_target_pairs={{0,1},{2,3},{4,5},{6,7},{8,9},{10,11},{12,13},{14,15},{16,17},{18,... | collective-permute-start | bytes 66104 | tf_op jit(solution)/shard_map/ppermute | solution.py:19
  179.5 5.1 %collective-permute-start.16 = (f32[9,34,18,1]{1,2,3,0:T(8,128)S(1)}, f32[9,34,18,1]{1,2,3,0:T(8,128)}, u32[]{:S(2)}, u32[]{:S(2)}) collective-permute-start(f32[9,34,18,1]{1,2,3,0:T(8,128)S(1)} %copy.211), channel_id=1, source_target_pairs={{1,0},{3,2},{5,4},{7,6},{9,8},{11,10},{13,12},{15,14},{17,16},{19,... | collective-permute-start | bytes 66104 | tf_op jit(solution)/shard_map/ppermute | solution.py:21
